TPU v7x, 32 devices: a whole 2x2x4 slice. The times are simulated.
32 devices in a mesh: band: 4 (over y, x), pulse: 2 (over core), range: 4 (over z).
Axes of the slice: x: 2, y: 2, z: 4, core: 2. Of those that a mesh axis runs over, the one named last changes fastest.
Arguments:
- echoes: bfloat16 [4, 2, 8192, 4096], P('band', None, 'pulse', 'range'), may hold values from -6 to 6
- range_phase: float32 [4, 4096], P('band'), may hold values from -3.140625 to 3.140625
- pulse_shift: int32 [4, 8192], P('band', ('pulse', 'range')), may hold values from -64 to 64
- bin_offset: int32 [4], replicated, may hold values from 0 to 1024, as said below
- doppler_phase: float32 [8192], replicated, may hold values from -3.140625 to 3.140625
Outputs:
- focused: bfloat16 [12288, 2, 8192], P(('band', 'pulse', 'range'))
Inputs may be any that keep to these rules, and one draw needn't show every extreme that they name: Band b's spectrum begins at combined bin b * 3072 - 2 * 512 + bin_offset[b]. In every draw some band other than the last has offset 2 * 512 and the band after it has offset 0.
All inputs are finite; a program needn't handle non-finite values.
Results may differ from a plain program's by a relative error of at most 0.0054.
Values may be sent and summed in bfloat16 or wider, within the bound.
A program may use at most 192 MiB of HBM per device.

v0:
```python
import math

import jax
import jax.numpy as jnp
from jax import lax
from jax.sharding import PartitionSpec as P

MARGIN = 512


def shifted(block, axis, distance):
    devices = range(lax.axis_size(axis))
    route = [(i - distance, i) for i in devices if i - distance in devices]
    return lax.ppermute(block, axis, route)


def split_length(length):
    outer_len = 1
    while outer_len * outer_len * 4 <= length and length % (outer_len * 2) == 0:
        outer_len = outer_len * 2
    return (outer_len, length // outer_len)


def twiddle_table(rows_count, cols_count, modulus, rotation):
    product = jnp.mod(
        jnp.arange(rows_count, dtype=jnp.int32)[:, None]
        * jnp.arange(cols_count, dtype=jnp.int32)[None, :],
        modulus,
    )
    angles = product.astype(jnp.float32) * (2.0 * math.pi / modulus)
    return (jnp.cos(angles), rotation * jnp.sin(angles))


def complex_contract(real_part, imag_part, table_real, table_imag, pattern):
    highest = lax.Precision.HIGHEST
    first = jnp.einsum(pattern, real_part, table_real, precision=highest)
    second = jnp.einsum(pattern, imag_part, table_imag, precision=highest)
    joined = jnp.einsum(pattern, real_part + imag_part, table_real + table_imag, precision=highest)
    return (first - second, joined - first - second)


def transform(real_part, imag_part, rotation):
    length = real_part.shape[-1]
    outer_len, inner_len = split_length(length)
    leading = real_part.shape[:-1]
    real_part = real_part.reshape(leading + (outer_len, inner_len))
    imag_part = imag_part.reshape(leading + (outer_len, inner_len))
    table_real, table_imag = twiddle_table(outer_len, outer_len, outer_len, rotation)
    real_part, imag_part = complex_contract(
        real_part, imag_part, table_real, table_imag, "...ab,ak->...kb"
    )
    twist_real, twist_imag = twiddle_table(outer_len, inner_len, length, rotation)
    real_part, imag_part = (
        real_part * twist_real - imag_part * twist_imag,
        real_part * twist_imag + imag_part * twist_real,
    )
    table_real, table_imag = twiddle_table(inner_len, inner_len, inner_len, rotation)
    real_part, imag_part = complex_contract(
        real_part, imag_part, table_real, table_imag, "...kb,bm->...mk"
    )
    factor = 1.0 / math.sqrt(length)
    return (
        real_part.reshape(leading + (length,)) * factor,
        imag_part.reshape(leading + (length,)) * factor,
    )


def body(echoes, range_phase, pulse_shift, bin_offset, doppler_phase):
    range_count = lax.axis_size("range")
    pulse_count = lax.axis_size("pulse")
    group_size = pulse_count * range_count
    band_rows = echoes.shape[2]
    cells_local = echoes.shape[3]
    n_local = band_rows // range_count
    cell_count = cells_local * range_count
    owned_bins = cell_count - 2 * MARGIN
    spill_len = 2 * MARGIN
    filter_real = jnp.cos(range_phase[0])
    filter_imag = jnp.sin(range_phase[0])
    rows_in = echoes[0].reshape(2, range_count, n_local, cells_local)
    received = lax.all_to_all(rows_in, "range", split_axis=1, concat_axis=3, tiled=True)
    real_part = received[0, 0].astype(jnp.float32)
    imag_part = received[1, 0].astype(jnp.float32)
    real_part, imag_part = transform(real_part, imag_part, -1.0)
    real_part, imag_part = (
        real_part * filter_real - imag_part * filter_imag,
        real_part * filter_imag + imag_part * filter_real,
    )
    spectrum = jnp.transpose(jnp.stack((real_part, imag_part), axis=0), (2, 0, 1))
    shifts = pulse_shift[0]
    cell_index = jnp.arange(cell_count, dtype=jnp.int32)
    angles = jnp.mod(cell_index[:, None] * shifts[None, :], cell_count).astype(jnp.float32) * (
        -2.0 * math.pi / cell_count
    )
    ramp_real = jnp.cos(angles)
    ramp_imag = jnp.sin(angles)
    real_part = spectrum[:, 0] * ramp_real - spectrum[:, 1] * ramp_imag
    imag_part = spectrum[:, 0] * ramp_imag + spectrum[:, 1] * ramp_real
    contrib = jnp.stack((real_part, imag_part), axis=1).astype(jnp.bfloat16)
    band_index = lax.axis_index("band")
    offset = jnp.sum(
        jnp.where(jnp.arange(bin_offset.shape[0], dtype=jnp.int32) == band_index, bin_offset, 0)
    )
    padded = jnp.pad(contrib, ((spill_len, spill_len), (0, 0), (0, 0)))
    own_rows = lax.dynamic_slice_in_dim(padded, 2 * spill_len - offset, owned_bins, 0).astype(
        jnp.float32
    )
    upper = lax.dynamic_slice_in_dim(padded, owned_bins + 2 * spill_len - offset, spill_len, 0)
    lower = lax.dynamic_slice_in_dim(padded, spill_len - offset, spill_len, 0)
    from_below = shifted(upper, "band", 1)
    from_above = shifted(lower, "band", -1)
    stitched = own_rows.at[:spill_len].add(from_below.astype(jnp.float32))
    stitched = stitched.at[owned_bins - spill_len :].add(from_above.astype(jnp.float32))
    stitched_half = stitched.astype(jnp.bfloat16)
    doppler_real = jnp.cos(doppler_phase)
    doppler_imag = jnp.sin(doppler_phase)
    bins_local = owned_bins // group_size
    blocks = stitched_half.reshape(group_size, bins_local, 2, n_local)
    samples = lax.all_to_all(blocks, ("pulse", "range"), split_axis=0, concat_axis=3, tiled=True)[0]
    real_part = samples[:, 0].astype(jnp.float32)
    imag_part = samples[:, 1].astype(jnp.float32)
    real_part, imag_part = transform(real_part, imag_part, -1.0)
    real_part, imag_part = (
        real_part * doppler_real - imag_part * doppler_imag,
        real_part * doppler_imag + imag_part * doppler_real,
    )
    real_part, imag_part = transform(real_part, imag_part, 1.0)
    return jnp.stack((real_part, imag_part), axis=1).astype(jnp.bfloat16)


def solution(mesh):
    in_specs = (
        P("band", None, "pulse", "range"),
        P("band", None),
        P("band", ("pulse", "range")),
        P(),
        P(),
    )
    out_specs = P(("band", "pulse", "range"), None, None)
    return jax.shard_map(body, mesh=mesh, in_specs=in_specs, out_specs=out_specs, check_vma=False)
```

profile of v0, /device:TPU:5, one launch (start us, length us, event | category | flops | bytes accessed | tf_op | source)
XLA Modules:
  0.0 1734.4 jit_solution(6404051856957122684)
XLA Ops:
  24.5 358.9 %all-to-all-done = bf16[2,4,1024,1024]{3,2,0,1:T(8,128)(2,1)} async-done(((bf16[2,4,1024,1024]{3,2,0,1:T(8,128)(2,1)}), bf16[2,4,1024,1024]{3,2,0,1:T(8,128)(2,1)}, u32[]{:S(2)}, u32[]{:S(2)}) %all-to-all-start) | async-done | bytes 16777248 | tf_op jit(solution)/shard_map/all_to_all | solution.py:81
  383.3 21.6 %copy.65 = bf16[2,4,1024,1024]{2,3,1,0:T(8,128)(2,1)} copy(bf16[2,4,1024,1024]{3,2,0,1:T(8,128)(2,1)} %all-to-all-done) | data formatting | bytes 33554432 | tf_op jit(solution)/shard_map/all_to_all | solution.py:81
  411.9 18.7 %fusion.54 = f32[64,1024,64]{1,0,2:T(8,128)} fusion(bf16[1024,64,64]{0,2,1:T(8,128)(2,1)S(1)} %bitcast.226), kind=kOutput, calls=%fused_computation.89 | convolution fusion | flops 3221286912 | bytes 25165824 | tf_op jit(solution)/shard_map/...ab,ak->...kb/dot_general | solution.py:37
  437.9 19.1 %fusion.56 = f32[64,1024,64]{1,0,2:T(8,128)} fusion(bf16[1024,64,64]{0,2,1:T(8,128)(2,1)S(1)} %bitcast.225), kind=kOutput, calls=%fused_computation.91 | convolution fusion | flops 3221282816 | bytes 25165824 | tf_op jit(solution)/shard_map/...ab,ak->...kb/dot_general | solution.py:36
  457.1 42.1 %fusion.235 = (f32[1024,64,64]{0,1,2:T(8,128)}, f32[1024,64,64]{0,1,2:T(8,128)}, f32[1024,64,64]{0,1,2:T(8,128)}) fusion(f32[64,64]{0,1:T(8,128)S(1)} %get-tuple-element.61, f32[64,64]{0,1:T(8,128)S(1)} %get-tuple-element.62, f32[64,1024,64]{1,0,2:T(8,128)} %fusion.54, f32[64,1024,64]{1,0,2:T(8,128)} %fusion.56, f32[1024,64,64]{0,2,1:T(8,128)} %convert_add_fusion), kind=kOutput, calls=%fused_computation.266 | convolution fusion | flops 3263234048 | bytes 100696064 | tf_op jit(solution)/shard_map/...ab,ak->...kb/dot_general | solution.py:38
  499.2 33.7 %fusion.15 = f32[64,1024,64]{1,0,2:T(8,128)} fusion(f32[1024,64,64]{0,1,2:T(8,128)} %get-tuple-element.39), kind=kOutput, calls=%fused_computation.29 | convolution fusion | flops 3221282816 | bytes 33554432 | tf_op jit(solution)/shard_map/...kb,bm->...mk/dot_general | solution.py:36
  532.8 33.8 %bitcast_subtract_fusion.1 = (f32[1024,64,64]{0,1,2:T(8,128)}, f32[64,1024,64]{1,0,2:T(8,128)}) fusion(f32[64,1024,64]{1,0,2:T(8,128)} %fusion.15, f32[1024,64,64]{0,1,2:T(8,128)} %get-tuple-element.40), kind=kOutput, calls=%fused_computation.21 | convolution fusion | flops 3225481216 | bytes 67108864 | tf_op jit(solution)/shard_map/...kb,bm->...mk/dot_general | solution.py:37
  566.7 33.6 %fusion.9 = f32[1024,64,64]{0,1,2:T(8,128)} fusion(f32[64,1024,64]{1,0,2:T(8,128)} %get-tuple-element.56, f32[64,1024,64]{1,0,2:T(8,128)S(1)} %copy-done, f32[1024,64,64]{0,1,2:T(8,128)} %get-tuple-element.38), kind=kOutput, calls=%fused_computation.18 | convolution fusion | flops 3229679616 | bytes 67108864 | tf_op jit(solution)/shard_map/...kb,bm->...mk/dot_general | solution.py:38
  600.3 15.4 copy.73
  615.7 19.4 %copy.71 = f32[1024,64,64]{0,2,1:T(8,128)} copy(f32[1024,64,64]{0,1,2:T(8,128)S(1)} %copy-done.1) | data formatting | bytes 33554432 | tf_op jit(solution)/shard_map/sub | solution.py:39
  635.0 17.2 fusion.7
  664.4 71.8 %subtract_convert_fusion = (bf16[4096,1,1024]{2,0,1:T(8,128)(2,1)}, bf16[4096,1,1024]{2,0,1:T(8,128)(2,1)}) fusion(f32[4096,2,1024]{2,0,1:T(8,128)S(1)} %maximum_bitcast_fusion, s32[1024]{0:T(1024)S(1)} %bitcast.240), kind=kLoop, calls=%fused_computation.34 | loop fusion | flops 92274688 | bytes 50335744 | tf_op jit(solution)/shard_map/convert.4
  736.2 22.5 %fusion.3 = bf16[6144,2,1024]{2,0,1:T(8,128)(2,1)} fusion(bf16[4096,1,1024]{2,0,1:T(8,128)(2,1)} %get-tuple-element.44, bf16[4096,1,1024]{2,0,1:T(8,128)(2,1)} %get-tuple-element.43), kind=kLoop, calls=%fused_computation.6 | loop fusion | flops 113246208 | bytes 41943040 | tf_op jit(solution)/shard_map/stack | solution.py:99
  775.5 14.6 dynamic-slice_convert_fusion
  790.1 71.8 %collective-permute-done = bf16[1024,2,1024]{2,0,1:T(8,128)(2,1)} collective-permute-done((bf16[1024,2,1024]{2,0,1:T(8,128)(2,1)}, bf16[1024,2,1024]{2,0,1:T(8,128)(2,1)}, u32[]{:S(2)}, u32[]{:S(2)}) %collective-permute-start) | collective-permute-done | bytes 4194336 | tf_op jit(solution)/shard_map/ppermute | solution.py:14
  872.0 77.9 %collective-permute-done.1 = bf16[1024,2,1024]{2,0,1:T(8,128)(2,1)} collective-permute-done((bf16[1024,2,1024]{2,0,1:T(8,128)(2,1)}, bf16[1024,2,1024]{2,0,1:T(8,128)(2,1)}, u32[]{:S(2)}, u32[]{:S(2)}) %collective-permute-start.1) | collective-permute-done | bytes 4194336 | tf_op jit(solution)/shard_map/ppermute | solution.py:14
  984.3 272.1 %all-to-all-done.1 = bf16[8,384,2,1024]{3,1,2,0:T(8,128)(2,1)} async-done(((bf16[8,384,2,1024]{3,1,2,0:T(8,128)(2,1)}), bf16[8,384,2,1024]{3,1,2,0:T(8,128)(2,1)}, u32[]{:S(2)}, u32[]{:S(2)}) %all-to-all-start.1) | async-done | bytes 12582944 | tf_op jit(solution)/shard_map/all_to_all | solution.py:119
  1256.4 16.6 copy.75
  1321.4 33.5 %fusion.234 = (f32[384,64,128]{2,1,0:T(8,128)}, f32[384,64,128]{2,1,0:T(8,128)}, f32[384,64,128]{2,1,0:T(8,128)}) fusion(f32[64,128]{1,0:T(8,128)S(1)} %get-tuple-element.63, f32[64,128]{1,0:T(8,128)S(1)} %get-tuple-element.64, f32[64,384,128]{2,0,1:T(8,128)} %fusion.95, f32[64,384,128]{2,0,1:T(8,128)} %fusion.101, bf16[384,64,128]{2,1,0:T(8,128)(2,1)} %copy.93, ...), kind=kOutput, calls=%fused_computation.265 | convolution fusion | flops 2456879104 | bytes 75563008 | tf_op jit(solution)/shard_map/...ab,ak->...kb/dot_general | solution.py:38
  1354.8 25.5 %fusion.42 = f32[128,384,64]{1,0,2:T(8,128)} fusion(f32[384,64,128]{2,1,0:T(8,128)} %get-tuple-element.36), kind=kOutput, calls=%fused_computation.74 | convolution fusion | flops 4832067584 | bytes 25165824 | tf_op jit(solution)/shard_map/...kb,bm->...mk/dot_general | solution.py:36
  1380.3 29.5 %bitcast_subtract_fusion.9 = (f32[384,128,64]{0,1,2:T(8,128)}, f32[128,384,64]{1,0,2:T(8,128)}) fusion(f32[128,384,64]{1,0,2:T(8,128)} %fusion.42, f32[384,64,128]{2,1,0:T(8,128)} %get-tuple-element.37), kind=kOutput, calls=%fused_computation.60 | convolution fusion | flops 4835229696 | bytes 50331648 | tf_op jit(solution)/shard_map/...kb,bm->...mk/dot_general | solution.py:37
  1409.9 30.7 %fusion.30 = f32[384,128,64]{0,1,2:T(8,128)} fusion(f32[128,384,64]{1,0,2:T(8,128)} %get-tuple-element.58, f32[128,384,64]{1,0,2:T(8,128)} %fusion.42, f32[384,64,128]{2,1,0:T(8,128)} %get-tuple-element.35), kind=kOutput, calls=%fused_computation.57 | convolution fusion | flops 4838391808 | bytes 50331648 | tf_op jit(solution)/shard_map/...kb,bm->...mk/dot_general | solution.py:38
  1440.6 16.6 copy.82
  1457.2 16.6 copy.80
  1473.8 21.7 %fusion.231 = (f32[384,64,128]{0,2,1:T(8,128)}, f32[384,64,128]{0,2,1:T(8,128)}, f32[384,64,128]{0,2,1:T(8,128)}) fusion(f32[64,128]{1,0:T(8,128)S(1)} %get-tuple-element.52, f32[64,128]{1,0:T(8,128)S(1)} %get-tuple-element.51, f32[384,64,128]{0,2,1:T(8,128)} %bitcast.230, f32[384,64,128]{0,2,1:T(8,128)} %bitcast.231), kind=kLoop, calls=%fused_computation.264 | loop fusion | flops 22020096 | bytes 62980096 | tf_op jit(solution)/shard_map/add | solution.py:38
  1508.2 16.8 fusion.90
  1537.8 17.2 fusion.99
  1567.9 33.2 %fusion.230 = (f32[384,64,128]{2,1,0:T(8,128)}, f32[384,64,128]{2,1,0:T(8,128)}, f32[384,64,128]{2,1,0:T(8,128)}) fusion(f32[64,128]{1,0:T(8,128)S(1)} %copy-done.3, f32[64,128]{1,0:T(8,128)S(1)} %get-tuple-element.64, f32[64,384,128]{2,0,1:T(8,128)} %fusion.90, f32[64,384,128]{2,0,1:T(8,128)} %fusion.99, f32[384,64,128]{2,1,0:T(8,128)} %copy.85), kind=kOutput, calls=%fused_computation.263 | convolution fusion | flops 2447437824 | bytes 75563008 | tf_op jit(solution)/shard_map/...ab,ak->...kb/dot_general | solution.py:38
  1601.1 25.5 %fusion.36 = f32[128,384,64]{1,0,2:T(8,128)} fusion(f32[384,64,128]{2,1,0:T(8,128)} %get-tuple-element.30), kind=kOutput, calls=%fused_computation.68 | convolution fusion | flops 4832067584 | bytes 25165824 | tf_op jit(solution)/shard_map/...kb,bm->...mk/dot_general | solution.py:36
  1626.6 29.5 %fusion.26 = (bf16[384,128,64]{0,1,2:T(8,128)(2,1)}, f32[128,384,64]{1,0,2:T(8,128)}) fusion(f32[128,384,64]{1,0,2:T(8,128)} %fusion.36, f32[384,64,128]{2,1,0:T(8,128)} %get-tuple-element.31), kind=kOutput, calls=%fused_computation.48 | convolution fusion | flops 4841504768 | bytes 44040192 | tf_op jit(solution)/shard_map/...kb,bm->...mk/dot_general | solution.py:37
  1656.1 30.9 %fusion.24 = bf16[384,128,64]{0,1,2:T(8,128)(2,1)} fusion(f32[128,384,64]{1,0,2:T(8,128)} %get-tuple-element.60, f32[128,384,64]{1,0,2:T(8,128)} %fusion.36, f32[384,64,128]{2,1,0:T(8,128)} %get-tuple-element.29), kind=kOutput, calls=%fused_computation.45 | convolution fusion | flops 4844666880 | bytes 44040192 | tf_op jit(solution)/shard_map/...kb,bm->...mk/dot_general | solution.py:38
  1703.2 31.0 %copy.91 = bf16[384,2,8192]{2,1,0:T(2,128)(2,1)} copy(bf16[384,2,8192]{0,2,1:T(8,128)(2,1)} %pad_maximum_fusion) | data formatting | bytes 25165824 | tf_op jit(solution)/shard_map/stack | solution.py:128
  (46 shorter events, 211.6 us)
Async XLA Ops:
  13.9 7.1 copy-start.7
  13.9 10.1 copy-start.5
  13.9 369.5 %all-to-all-start = ((bf16[2,4,1024,1024]{3,2,0,1:T(8,128)(2,1)}), bf16[2,4,1024,1024]{3,2,0,1:T(8,128)(2,1)}, u32[]{:S(2)}, u32[]{:S(2)}) async-start(bf16[2,4,1024,1024]{3,2,0,1:T(8,128)(2,1)} %copy.64), calls=%async_computation | async-start | bytes 33554432 | tf_op jit(solution)/shard_map/all_to_all | solution.py:81
  532.8 33.8 %copy-start = (f32[64,1024,64]{1,0,2:T(8,128)S(1)}, f32[64,1024,64]{1,0,2:T(8,128)}, u32[]{:S(2)}) copy-start(f32[64,1024,64]{1,0,2:T(8,128)} %fusion.15) | copy-start | bytes 50331652
  600.3 15.4 copy-start.1
  652.3 12.1 copy-start.6
  768.2 93.8 %collective-permute-start = (bf16[1024,2,1024]{2,0,1:T(8,128)(2,1)}, bf16[1024,2,1024]{2,0,1:T(8,128)(2,1)}, u32[]{:S(2)}, u32[]{:S(2)}) collective-permute-start(bf16[1024,2,1024]{2,0,1:T(8,128)(2,1)} %get-tuple-element.46), channel_id=1, source_target_pairs={{0,8},{8,16},{16,24},{1,9},{9,17},{17,25},{2,10},{10,18},{18,26},{... | collective-permute-start | bytes 12582920 | tf_op jit(solution)/shard_map/ppermute | solution.py:14
  771.3 178.6 %collective-permute-start.1 = (bf16[1024,2,1024]{2,0,1:T(8,128)(2,1)}, bf16[1024,2,1024]{2,0,1:T(8,128)(2,1)}, u32[]{:S(2)}, u32[]{:S(2)}) collective-permute-start(bf16[1024,2,1024]{2,0,1:T(8,128)(2,1)} %get-tuple-element.45), channel_id=1, source_target_pairs={{8,0},{16,8},{24,16},{9,1},{17,9},{25,17},{10,2},{18,10},{26,18},{... | collective-permute-start | bytes 12582920 | tf_op jit(solution)/shard_map/ppermute | solution.py:14
  975.2 8.9 copy-start.4
  975.2 281.1 %all-to-all-start.1 = ((bf16[8,384,2,1024]{3,1,2,0:T(8,128)(2,1)}), bf16[8,384,2,1024]{3,1,2,0:T(8,128)(2,1)}, u32[]{:S(2)}, u32[]{:S(2)}) async-start(bf16[8,384,2,1024]{3,1,2,0:T(8,128)(2,1)} %copy.74), calls=%async_computation.1 | async-start | bytes 25165824 | tf_op jit(solution)/shard_map/all_to_all | solution.py:119
  1555.1 12.8 copy-start.3
  1687.0 6.7 copy-start.2
where the time goes:
time: 1750 us; the launch traced here: 1730 us
  waiting for transfers between devices  781 us (45%)
  matrix products  473 us (27%)
  local copies, waits for them, and re-layouts  250 us (14%)
  other arithmetic  205 us (12%)
  starting transfers between devices  21.3 us (1%)
    all_to_all x1, waiting for transfers between devices, body(): lax.all_to_all(rows_in, 'range', split_axis=1, concat_axis=3, tiled=True)  359 us
    all_to_all x1, waiting for transfers between devices, body(): lax.all_to_all(blocks, ('pulse', 'range'), split_axis=0, concat_axis=3, t...  272 us
    dot_general x6, matrix products, complex_contract(): jnp.einsum(pattern, real_part + imag_part, table_real + table_imag, preci...  204 us
    ppermute x2, waiting for transfers between devices, shifted(): return lax.ppermute(block, axis, route)  150 us
    dot_general x6, matrix products, complex_contract(): second = jnp.einsum(pattern, imag_part, table_imag, precision=highest)  138 us
    dot_general x6, matrix products, complex_contract(): first = jnp.einsum(pattern, real_part, table_real, precision=highest)  131 us
    another operation x1, other arithmetic  71.8 us
    sub x4, local copies, waits for them, and re-layouts, complex_contract(): return (first - second, joined - first - second)  68 us
  transfers between devices with their start and end apart: 4, of which 4 were waited for; matrix products, arithmetic and copies ran while one was open for 2% of the time, Pallas kernels for 0%

commit v1 on v0

v1 whole, which is shorter than its diff:
```python
import functools
import math

import jax
import jax.numpy as jnp
import numpy as np
from jax import lax
from jax.experimental import pallas as pl
from jax.experimental.pallas import tpu as pltpu
from jax.sharding import PartitionSpec as P

MARGIN = 512
SHIFT_MAX = 64
LANES = 128


def shifted(block, axis, distance):
    devices = range(lax.axis_size(axis))
    route = [(i - distance, i) for i in devices if i - distance in devices]
    return lax.ppermute(block, axis, route)


def phases(rows, cols, modulus):
    product = np.arange(rows)[:, None] * np.arange(cols)[None, :] % modulus
    angles = product * (2.0 * np.pi / modulus)
    return np.cos(angles), np.sin(angles)


def high_low(table):
    high = table.astype(jnp.bfloat16)
    low = (table - high.astype(np.float64)).astype(jnp.bfloat16)
    return high, low


def left_table(length, rotation, order_in=None):
    cos, sin = phases(length, length, length)
    sin = rotation * sin
    full = np.block([[cos, -sin], [sin, cos]])
    if order_in is not None:
        full = full[:, order_in]
    return np.concatenate(high_low(full), axis=0)


def right_table(length, rotation):
    cos, sin = phases(length, length, length)
    sin = rotation * sin
    return np.stack(high_low(np.block([[cos, sin], [-sin, cos]])))


def twist_table(rows, length, rotation):
    cos, sin = phases(rows, LANES, length)
    return (np.stack((cos, rotation * sin)) / math.sqrt(length)).astype(np.float32)


def source_order(sources, rows):
    index = np.arange(2 * sources * rows).reshape(2, sources, rows)
    return index.transpose(1, 0, 2).reshape(-1)


def dot(left, right):
    return jnp.dot(left, right, preferred_element_type=jnp.float32)


def rotated(real, imag, by_real, by_imag):
    return real * by_real - imag * by_imag, real * by_imag + imag * by_real


def gathered(ref, index):
    return jnp.concatenate([ref[s, index] for s in range(ref.shape[0])], axis=0)


def range_kernel(shift_ref, x_ref, left_ref, twist_ref, right_ref, turn_ref, o_ref):
    count = x_ref.shape[1]
    outer = twist_ref.shape[1]
    first = pl.program_id(0) * count
    left = left_ref[...]
    highs, lows = [], []
    for g in range(count):
        y = dot(left, gathered(x_ref, g))
        y = y[: 2 * outer] + y[2 * outer :]
        zr, zi = rotated(y[:outer], y[outer:], twist_ref[0], twist_ref[1])
        z = jnp.concatenate((zr, zi), axis=1)
        high = z.astype(jnp.bfloat16)
        highs.append(high)
        lows.append((z - high.astype(jnp.float32)).astype(jnp.bfloat16))
    high = jnp.concatenate(highs, axis=0)
    low = jnp.concatenate(lows, axis=0)
    s = dot(high, right_ref[0]) + dot(low, right_ref[0]) + dot(high, right_ref[1])
    for g in range(count):
        shift = shift_ref[first + g] + SHIFT_MAX
        part = s[g * outer : (g + 1) * outer]
        cr, ci = rotated(part[:, :LANES], part[:, LANES:], turn_ref[shift, 0], turn_ref[shift, 1])
        o_ref[g, 0] = cr.astype(jnp.bfloat16)
        o_ref[g, 1] = ci.astype(jnp.bfloat16)


def azimuth_kernel(
    x_ref, left_ref, twist_ref, right_ref, phase_ref, back_ref, untwist_ref, last_ref, o_ref
):
    count = x_ref.shape[1]
    outer = twist_ref.shape[1]
    left = left_ref[...]
    rows = []
    for g in range(count):
        y = dot(left, gathered(x_ref, g))
        y = y[: 2 * outer] + y[2 * outer :]
        zr, zi = rotated(y[:outer], y[outer:], twist_ref[0], twist_ref[1])
        rows.append(jnp.concatenate((zr, zi), axis=1).astype(jnp.bfloat16))
    z = jnp.concatenate(rows, axis=0)
    d = dot(z, right_ref[0]) + dot(z, right_ref[1])
    rows = []
    for g in range(count):
        part = d[g * outer : (g + 1) * outer]
        dr, di = rotated(part[:, :LANES], part[:, LANES:], phase_ref[0], phase_ref[1])
        rows.append(jnp.concatenate((dr, di), axis=1).astype(jnp.bfloat16))
    z = jnp.concatenate(rows, axis=0)
    d = dot(z, back_ref[0]) + dot(z, back_ref[1])
    last = last_ref[...]
    for g in range(count):
        part = d[g * outer : (g + 1) * outer]
        er, ei = rotated(part[:, :LANES], part[:, LANES:], untwist_ref[0], untwist_ref[1])
        e = jnp.concatenate((er, ei), axis=0).astype(jnp.bfloat16)
        y = dot(last, e)
        y = y[: 2 * outer] + y[2 * outer :]
        o_ref[g, 0] = y[:outer].astype(jnp.bfloat16)
        o_ref[g, 1] = y[outer:].astype(jnp.bfloat16)


def whole_spec(array):
    return pl.BlockSpec(array.shape, lambda i, *_: (0,) * array.ndim)


def run(kernel, name, tables, x, outer, block, scalars=()):
    sources, total, rows, _ = x.shape
    block = math.gcd(block, total)
    grid_spec = pltpu.PrefetchScalarGridSpec(
        num_scalar_prefetch=len(scalars),
        grid=(total // block,),
        in_specs=[pl.BlockSpec((sources, block, rows, LANES), lambda i, *_: (0, i, 0, 0))]
        + [whole_spec(t) for t in tables],
        out_specs=pl.BlockSpec((block, 2, outer, LANES), lambda i, *_: (i, 0, 0, 0)),
    )
    elements = total * outer * LANES
    return pl.pallas_call(
        kernel,
        grid_spec=grid_spec,
        out_shape=jax.ShapeDtypeStruct((total, 2, outer, LANES), jnp.bfloat16),
        compiler_params=pltpu.CompilerParams(vmem_limit_bytes=48 * 1024 * 1024),
        cost_estimate=pl.CostEstimate(
            flops=elements * 4096, bytes_accessed=elements * 8, transcendentals=0
        ),
        name=name,
    )(*scalars, x, *tables)


def packed_rows(x):
    sources, total, rows, lanes = x.shape
    if rows % 16 == 0:
        return x
    return x.transpose(1, 0, 2, 3).reshape(1, total, sources * rows, lanes)


def body(echoes, range_phase, pulse_shift, bin_offset, doppler_phase):
    range_count = lax.axis_size("range")
    pulse_count = lax.axis_size("pulse")
    group_size = pulse_count * range_count
    band_rows = echoes.shape[2]
    cells_local = echoes.shape[3]
    n_local = band_rows // range_count
    cell_count = cells_local * range_count
    owned_bins = cell_count - 2 * MARGIN
    spill_len = 2 * MARGIN
    pulses = band_rows * pulse_count

    outer = cell_count // LANES
    part_rows = cells_local // LANES
    rows_in = echoes[0].reshape(2, range_count, n_local, part_rows, LANES)
    rows_in = rows_in.transpose(1, 2, 0, 3, 4).reshape(range_count, n_local, 2 * part_rows, LANES)
    received = lax.all_to_all(rows_in, "range", split_axis=0, concat_axis=0, tiled=True)
    shifts = jnp.arange(-SHIFT_MAX, SHIFT_MAX + 1, dtype=jnp.int32)
    cell_index = (
        jnp.arange(outer, dtype=jnp.int32)[:, None]
        + outer * jnp.arange(LANES, dtype=jnp.int32)[None, :]
    )
    angles = jnp.mod(cell_index[None] * shifts[:, None, None], cell_count).astype(jnp.float32) * (
        -2.0 * math.pi / cell_count
    )
    filter_phase = range_phase[0].reshape(LANES, outer).T
    turn_real, turn_imag = rotated(
        jnp.cos(angles), jnp.sin(angles), jnp.cos(filter_phase), jnp.sin(filter_phase)
    )
    tables = [
        jnp.asarray(left_table(outer, -1.0, source_order(range_count, part_rows))),
        jnp.asarray(twist_table(outer, cell_count, -1.0)),
        jnp.asarray(right_table(LANES, -1.0)),
        jnp.stack((turn_real, turn_imag), axis=1),
    ]
    spectrum = run(
        range_kernel, "range", tables, packed_rows(received), outer, 16, (pulse_shift[0],)
    )
    fold = n_local // LANES
    contrib = spectrum.reshape(fold, LANES, 2, outer, LANES).transpose(4, 3, 2, 0, 1)
    contrib = contrib.reshape(cell_count, 2 * fold, LANES)

    band_index = lax.axis_index("band")
    offset = jnp.sum(
        jnp.where(jnp.arange(bin_offset.shape[0], dtype=jnp.int32) == band_index, bin_offset, 0)
    )
    padded = jnp.pad(contrib, ((spill_len, spill_len), (0, 0), (0, 0)))
    upper = lax.dynamic_slice_in_dim(padded, owned_bins + 2 * spill_len - offset, spill_len, 0)
    lower = lax.dynamic_slice_in_dim(padded, spill_len - offset, spill_len, 0)
    from_below = shifted(upper, "band", 1)
    from_above = shifted(lower, "band", -1)
    own = lax.dynamic_slice_in_dim(padded, 2 * spill_len - offset, owned_bins, 0)
    rest = ((0, 0), (0, 0))
    stitched = (
        own.astype(jnp.float32)
        + jnp.pad(from_below, ((0, owned_bins - spill_len),) + rest).astype(jnp.float32)
        + jnp.pad(from_above, ((owned_bins - spill_len, 0),) + rest).astype(jnp.float32)
    ).astype(jnp.bfloat16)

    bins_local = owned_bins // group_size
    outer = pulses // LANES
    blocks = stitched.reshape(group_size, bins_local, 2 * fold, LANES)
    samples = lax.all_to_all(blocks, ("pulse", "range"), split_axis=0, concat_axis=0, tiled=True)
    doppler = doppler_phase.reshape(LANES, outer).T
    tables = [
        jnp.asarray(left_table(outer, -1.0, source_order(group_size, fold))),
        jnp.asarray(twist_table(outer, pulses, -1.0)),
        jnp.asarray(right_table(LANES, -1.0)),
        jnp.stack((jnp.cos(doppler), jnp.sin(doppler))),
        jnp.asarray(right_table(LANES, 1.0)),
        jnp.asarray(twist_table(outer, pulses, 1.0)),
        jnp.asarray(left_table(outer, 1.0)),
    ]
    focused = run(azimuth_kernel, "azimuth", tables, packed_rows(samples), outer, 8)
    return focused.reshape(bins_local, 2, pulses)


def solution(mesh):
    in_specs = (
        P("band", None, "pulse", "range"),
        P("band", None),
        P("band", ("pulse", "range")),
        P(),
        P(),
    )
    out_specs = P(("band", "pulse", "range"), None, None)
    return jax.shard_map(body, mesh=mesh, in_specs=in_specs, out_specs=out_specs, check_vma=False)
```

time: 1750 us -> 1060 us (0.61)
  matrix products: 473 us -> 0 us
  other arithmetic: 205 us -> 29.5 us
  local copies, waits for them, and re-layouts: 250 us -> 100 us
  Pallas kernels: 0 us -> 105 us
    dot_general x18 -> x0, matrix products: 473 us -> none  [the longest x6 204 us: complex_contract(): jnp.einsum(pattern, real_part + imag_part, table_real + table_imag, preci...]
    pallas_call x0 -> x2, Pallas kernels: none -> 105 us  [run(): pl.pallas_call(kernel, grid_spec=grid_spec, out_shape=jax.ShapeDtypeStruc...]
    another operation x3 -> x2, other arithmetic: 100 us -> 2.62 us  [the longest x1 2.6 us: body(): jnp.stack((turn_real, turn_imag), axis=1)]
    sub x5 -> x0, local copies, waits for them, and re-layouts: 80.7 us -> none  [the longest x4 68 us: complex_contract(): return (first - second, joined - first - second)]
    transpose x0 -> x1, local copies, waits for them, and re-layouts: none -> 54 us  [body(): spectrum.reshape(fold, LANES, 2, outer, LANES).transpose(4, 3, 2, 0, 1)]
    another operation x4 -> x1, local copies, waits for them, and re-layouts: 55.3 us -> 7.44 us  [body(): rows_in = echoes[0].reshape(2, range_count, n_local, part_rows, LANES)]
    all_to_all x2 -> x0, local copies, waits for them, and re-layouts: 38.2 us -> none  [the longest x1 21.6 us: body(): lax.all_to_all(rows_in, 'range', split_axis=1, concat_axis=3, tiled=True)]
    add x2, other arithmetic: 29.1 us -> 0.01 us  [the longest x1 0.01 us: body(): jnp.arange(outer, dtype=jnp.int32)[:, None]]
  transfers between devices with their start and end apart: 4 -> 4, of which waited for: 4 -> 4; matrix products, arithmetic and copies ran while one was open for 2% -> 1% of each run, Pallas kernels for 0% -> 0%
where the time goes in v1:
time: 1060 us; the launch traced here: 1050 us
  waiting for transfers between devices  795 us (75%)
  Pallas kernels  105 us (10%)
  local copies, waits for them, and re-layouts  100 us (9%)
  other arithmetic  29.5 us (3%)
  starting transfers between devices  21.8 us (2%)
    all_to_all x1, waiting for transfers between devices, body(): lax.all_to_all(rows_in, 'range', split_axis=0, concat_axis=0, tiled=True)  347 us
    all_to_all x1, waiting for transfers between devices, body(): lax.all_to_all(blocks, ('pulse', 'range'), split_axis=0, concat_axis=0, t...  273 us
    ppermute x2, waiting for transfers between devices, shifted(): return lax.ppermute(block, axis, route)  175 us
    pallas_call x2, Pallas kernels, run(): pl.pallas_call(kernel, grid_spec=grid_spec, out_shape=jax.ShapeDtypeStruc...  105 us
    transpose x1, local copies, waits for them, and re-layouts, body(): spectrum.reshape(fold, LANES, 2, outer, LANES).transpose(4, 3, 2, 0, 1)  54 us
  transfers between devices with their start and end apart: 4, of which 4 were waited for; matrix products, arithmetic and copies ran while one was open for 1% of the time, Pallas kernels for 0%

profile of v1, /device:TPU:5, one launch (start us, length us, event | category | flops | bytes accessed | tf_op | source)
XLA Modules:
  0.0 1054.8 jit_solution(5743283106932124167)
XLA Ops:
  0.0 10.2 copy.25
  10.2 7.4 copy.27
  17.7 7.1 all-to-all-start
  24.8 0.5 cosine_reduce_fusion
  25.3 0.1 sin.36
  25.4 0.1 copy.21
  25.5 0.1 cos.36
  25.6 0.1 copy.20
  25.6 0.7 fusion.5
  28.6 8.7 multiply_subtract_fusion
  37.3 0.0 copy-start.2
  37.3 0.0 copy-start.8
  37.3 2.6 pad_maximum_fusion.turn_ref
  39.9 347.2 %all-to-all-done.x_ref = bf16[4,1024,16,128]{3,2,1,0:T(8,128)(2,1)} async-done(((bf16[4,1024,16,128]{3,2,1,0:T(8,128)(2,1)}), bf16[4,1024,16,128]{3,2,1,0:T(8,128)(2,1)}, u32[]{:S(2)}, u32[]{:S(2)}) %all-to-all-start) | async-done | bytes 16777248 | tf_op jit(solution)/shard_map/all_to_all | solution.py:179
  387.2 2.2 copy-done
  389.4 53.3 %range.1 = bf16[1024,2,32,128]{3,2,1,0:T(8,128)(2,1)} custom-call(s32[1024]{0:T(1024)S(1)} %bitcast.26, bf16[4,1024,16,128]{3,2,1,0:T(8,128)(2,1)} %all-to-all-done.x_ref, bf16[128,64]{1,0:T(8,128)(2,1)S(1)} %copy-done.8, f32[2,32,128]{2,1,0:T(8,128)S(1)} %copy-done.9, bf16[2,256,256]{2,1,0:T(8,128)(2,1)S(1)} %copy-done.2, f32[129,2,32,128]{3,2,1,0:T(8,128)S(1)} %copy-done), custom_call_target="tpu_custom_call" | custom-call | flops 17179869184 | bytes 33554432 | tf_op jit(solution)/shard_map/range/pallas_call | solution.py:144
  442.6 54.0 %copy.22 = bf16[128,32,2,8,128]{4,3,2,1,0:T(8,128)(2,1)} copy(bf16[128,32,2,8,128]{0,1,2,4,3:T(8,128)(2,1)} %bitcast.33) | data formatting | bytes 33554432 | tf_op jit(solution)/shard_map/transpose | solution.py:202
  496.6 7.1 pad_dynamic-slice_fusion.1
  503.7 3.1 collective-permute-start.1
  506.8 4.1 collective-permute-start
  512.0 84.5 %collective-permute-done.1 = bf16[1024,16,128]{2,1,0:T(8,128)(2,1)} collective-permute-done((bf16[1024,16,128]{2,1,0:T(8,128)(2,1)}, bf16[1024,16,128]{2,1,0:T(8,128)(2,1)}, u32[]{:S(2)}, u32[]{:S(2)}) %collective-permute-start.1) | collective-permute-done | bytes 4194336 | tf_op jit(solution)/shard_map/ppermute | solution.py:20
  596.6 90.3 %collective-permute-done = bf16[1024,16,128]{2,1,0:T(8,128)(2,1)} collective-permute-done((bf16[1024,16,128]{2,1,0:T(8,128)(2,1)}, bf16[1024,16,128]{2,1,0:T(8,128)(2,1)}, u32[]{:S(2)}, u32[]{:S(2)}) %collective-permute-start) | collective-permute-done | bytes 4194336 | tf_op jit(solution)/shard_map/ppermute | solution.py:20
  686.8 17.5 %add_convert_fusion = bf16[3072,16,128]{2,1,0:T(8,128)(2,1)} fusion(s32[]{:T(128)S(6)} %select_n.39, bf16[4096,16,128]{2,1,0:T(8,128)(2,1)} %bitcast.28, bf16[1024,16,128]{2,1,0:T(8,128)(2,1)} %collective-permute-done.1, bf16[1024,16,128]{2,1,0:T(8,128)(2,1)} %collective-permute-done), kind=kLoop, calls=%fused_computation.3 | loop fusion | flops 37748736 | bytes 37748740 | tf_op jit(solution)/shard_map/convert_element_type | solution.py:220
  704.4 7.5 all-to-all-start.1
  711.9 0.1 fusion.6
  712.0 0.1 sin.39
  712.1 0.1 copy.24
  712.2 0.1 cos.39
  712.3 0.1 copy.23
  712.4 272.7 %all-to-all-done.1.x_ref = bf16[8,384,16,128]{3,2,1,0:T(8,128)(2,1)} async-done(((bf16[8,384,16,128]{3,2,1,0:T(8,128)(2,1)}), bf16[8,384,16,128]{3,2,1,0:T(8,128)(2,1)}, u32[]{:S(2)}, u32[]{:S(2)}) %all-to-all-start.1) | async-done | bytes 12582944 | tf_op jit(solution)/shard_map/all_to_all | solution.py:225
  985.1 51.7 %azimuth.1 = bf16[384,2,64,128]{3,2,1,0:T(8,128)(2,1)} custom-call(bf16[8,384,16,128]{3,2,1,0:T(8,128)(2,1)} %all-to-all-done.1.x_ref, bf16[256,128]{1,0:T(8,128)(2,1)S(1)} %copy-done.4, f32[2,64,128]{2,1,0:T(8,128)S(1)} %copy-done.5, bf16[2,256,256]{2,1,0:T(8,128)(2,1)S(1)} %copy-done.2, f32[2,64,128]{2,1,0:T(8,128)S(1)} %pad_maximum_fusion.1.phase_ref, ...), custom_call_target="tpu_custom_call" | custom-call | flops 12884901888 | bytes 25165824 | tf_op jit(solution)/shard_map/azimuth/pallas_call | solution.py:144
  1036.8 18.0 %reshape.133 = bf16[384,2,8192]{2,1,0:T(2,128)(2,1)} reshape(bf16[384,2,64,128]{3,2,1,0:T(8,128)(2,1)} %azimuth.1) | data formatting | bytes 25165824 | tf_op jit(solution)/shard_map/reshape | solution.py:237
  (27 shorter events, 0.1 us)
Async XLA Ops:
  17.6 7.1 copy-start.11
  17.7 8.0 copy-start.12
  17.7 369.5 %all-to-all-start = ((bf16[4,1024,16,128]{3,2,1,0:T(8,128)(2,1)}), bf16[4,1024,16,128]{3,2,1,0:T(8,128)(2,1)}, u32[]{:S(2)}, u32[]{:S(2)}) async-start(bf16[4,1024,16,128]{3,2,1,0:T(8,128)(2,1)} %bitcast.29), calls=%async_computation | async-start | bytes 33554432 | tf_op jit(solution)/shard_map/all_to_all | solution.py:179
  37.3 349.9 %copy-start.1 = (s32[1,1024]{1,0:T(1,128)S(1)}, s32[1,1024]{1,0:T(1,128)}, u32[]{:S(2)}) copy-start(s32[1,1024]{1,0:T(1,128)} %param.16) | copy-start | bytes 12292
  37.3 349.9 %copy-start.2 = (bf16[2,256,256]{2,1,0:T(8,128)(2,1)S(1)}, bf16[2,256,256]{2,1,0:T(8,128)(2,1)}, u32[]{:S(2)}) copy-start(bf16[2,256,256]{2,1,0:T(8,128)(2,1)} %constant.60.clone.right_ref) | copy-start | bytes 786436
  37.3 349.8 %copy-start.8 = (bf16[128,64]{1,0:T(8,128)(2,1)S(1)}, bf16[128,64]{1,0:T(8,128)(2,1)}, u32[]{:S(2)}) copy-start(bf16[128,64]{1,0:T(8,128)(2,1)} %constant.58.clone.left_ref) | copy-start | bytes 49156
  37.3 349.8 %copy-start.9 = (f32[2,32,128]{2,1,0:T(8,128)S(1)}, f32[2,32,128]{2,1,0:T(8,128)}, u32[]{:S(2)}) copy-start(f32[2,32,128]{2,1,0:T(8,128)} %constant.59.clone.twist_ref) | copy-start | bytes 98308
  387.2 2.2 copy-start
  503.7 92.9 %collective-permute-start.1 = (bf16[1024,16,128]{2,1,0:T(8,128)(2,1)}, bf16[1024,16,128]{2,1,0:T(8,128)(2,1)}, u32[]{:S(2)}, u32[]{:S(2)}) collective-permute-start(bf16[1024,16,128]{2,1,0:T(8,128)(2,1)} %get-tuple-element.8), channel_id=1, source_target_pairs={{8,0},{16,8},{24,16},{9,1},{17,9},{25,17},{10,2},{18,10},{26,18},{... | collective-permute-start | bytes 12582920 | tf_op jit(solution)/shard_map/ppermute | solution.py:20
  506.8 180.0 %collective-permute-start = (bf16[1024,16,128]{2,1,0:T(8,128)(2,1)}, bf16[1024,16,128]{2,1,0:T(8,128)(2,1)}, u32[]{:S(2)}, u32[]{:S(2)}) collective-permute-start(bf16[1024,16,128]{2,1,0:T(8,128)(2,1)} %get-tuple-element.7), channel_id=1, source_target_pairs={{0,8},{8,16},{16,24},{1,9},{9,17},{17,25},{2,10},{10,18},{18,26},{... | collective-permute-start | bytes 12582920 | tf_op jit(solution)/shard_map/ppermute | solution.py:20
  704.4 7.6 copy-start.10
  704.4 280.7 %copy-start.3 = (bf16[2,256,256]{2,1,0:T(8,128)(2,1)S(1)}, bf16[2,256,256]{2,1,0:T(8,128)(2,1)}, u32[]{:S(2)}) copy-start(bf16[2,256,256]{2,1,0:T(8,128)(2,1)} %constant.63.clone.back_ref) | copy-start | bytes 786436
  704.4 280.7 %copy-start.4 = (bf16[256,128]{1,0:T(8,128)(2,1)S(1)}, bf16[256,128]{1,0:T(8,128)(2,1)}, u32[]{:S(2)}) copy-start(bf16[256,128]{1,0:T(8,128)(2,1)} %constant.61.clone.left_ref) | copy-start | bytes 196612
  704.4 280.7 %copy-start.5 = (f32[2,64,128]{2,1,0:T(8,128)S(1)}, f32[2,64,128]{2,1,0:T(8,128)}, u32[]{:S(2)}) copy-start(f32[2,64,128]{2,1,0:T(8,128)} %constant.62.clone.twist_ref) | copy-start | bytes 196612
  704.4 280.7 %copy-start.6 = (f32[2,64,128]{2,1,0:T(8,128)S(1)}, f32[2,64,128]{2,1,0:T(8,128)}, u32[]{:S(2)}) copy-start(f32[2,64,128]{2,1,0:T(8,128)} %constant.64.clone.untwist_ref) | copy-start | bytes 196612
  704.4 280.7 %copy-start.7 = (bf16[256,128]{1,0:T(8,128)(2,1)S(1)}, bf16[256,128]{1,0:T(8,128)(2,1)}, u32[]{:S(2)}) copy-start(bf16[256,128]{1,0:T(8,128)(2,1)} %constant.65.clone.last_ref) | copy-start | bytes 196612
  704.4 280.7 %all-to-all-start.1 = ((bf16[8,384,16,128]{3,2,1,0:T(8,128)(2,1)}), bf16[8,384,16,128]{3,2,1,0:T(8,128)(2,1)}, u32[]{:S(2)}, u32[]{:S(2)}) async-start(bf16[8,384,16,128]{3,2,1,0:T(8,128)(2,1)} %bitcast.31), calls=%async_computation.1 | async-start | bytes 25165824 | tf_op jit(solution)/shard_map/all_to_all | solution.py:225
